TPU v7x, 32 devices: a whole 2x2x4 slice. The times are simulated.
32 devices in a mesh: dp: 8 (over z, y), tensor: 4 (over x, core).
Axes of the slice: x: 2, y: 2, z: 4, core: 2. Of those that a mesh axis runs over, the one named last changes fastest.
Arguments:
- tokens: bfloat16 [3, 4096, 1536], P(None, ('dp', 'tensor')), may hold values from -6 to 6
- lengths: int32 [3, 32, 6], P(None, ('dp', 'tensor')), may hold values from 1 to 64, 128 in all within a row
- first_gain: bfloat16 [1536], P(('dp', 'tensor')), may hold values from 0.099609375 to 1.8984375
- query_weight: bfloat16 [1536, 1536], P(('dp', 'tensor')), may hold values from -0.15625 to 0.15625
- key_weight: bfloat16 [1536, 768], P(('dp', 'tensor')), may hold values from -0.15625 to 0.15625
- value_weight: bfloat16 [1536, 768], P(('dp', 'tensor')), may hold values from -0.15625 to 0.15625
- output_weight: bfloat16 [1536, 1536], P(('dp', 'tensor')), may hold values from -0.4375 to 0.4375
- second_gain: bfloat16 [1536], P(('dp', 'tensor')), may hold values from 0.099609375 to 1.8984375
- gate_weight: bfloat16 [1536, 4096], P('dp', 'tensor'), may hold values from -0.15625 to 0.15625
- up_weight: bfloat16 [1536, 4096], P('dp', 'tensor'), may hold values from -0.15625 to 0.15625
- down_weight: bfloat16 [4096, 1536], P('tensor', 'dp'), may hold values from -0.09375 to 0.09375
- cotangent: bfloat16 [3, 4096, 1536], P(None, ('dp', 'tensor')), may hold values from -6 to 6
Outputs:
- layer_out: bfloat16 [3, 4096, 1536], P(None, ('dp', 'tensor'))
- input_grad: float32 [3, 4096, 1536], P(None, ('dp', 'tensor'))
- first_gain_grad: float32 [1536], P(('dp', 'tensor'))
- query_grad: float32 [1536, 1536], P(('dp', 'tensor'))
- key_grad: float32 [1536, 768], P(('dp', 'tensor'))
- value_grad: float32 [1536, 768], P(('dp', 'tensor'))
- output_grad: float32 [1536, 1536], P(('dp', 'tensor'))
- second_gain_grad: float32 [1536], P(('dp', 'tensor'))
- gate_grad: float32 [1536, 4096], P('dp', 'tensor')
- up_grad: float32 [1536, 4096], P('dp', 'tensor')
- down_grad: float32 [4096, 1536], P('tensor', 'dp')
Inputs may be any that keep to these rules, and one draw needn't show every extreme that they name: Row lengths[m, p] splits the 128 rows of pack p of micro-batch m into 6 runs in order, summing to 128; the first 5 runs are sequences, the last is padding; no run is longer than 64 rows.
All inputs are finite; a program needn't handle non-finite values.
Results may differ from a plain program's by a relative error of at most 0.013.
Values may be sent and summed in bfloat16 or wider, within the bound.
No kernel may reach another device: no remote copies, remote signals or barrier semaphores. Data moves between devices by JAX's collectives and lax.ppermute only.
A program may use at most 192 MiB of HBM per device.

v0:
```python
import math
import jax
import jax.numpy as jnp
from jax import lax
from jax.sharding import PartitionSpec as P

HEADS = 16
KV_HEADS = 8
HEAD = 96
SLOTS = 6
EPSILON = 1e-05
ROPE_BASE = 100000.0
NEG_LARGE = -1e30


def pack_layout(seq_lengths, row_count):
    seq_ends = jnp.cumsum(seq_lengths)
    seq_starts = seq_ends - seq_lengths
    row_index = jnp.arange(row_count, dtype=jnp.int32)
    segment = jnp.sum((row_index[:, None] >= seq_ends[None, :]).astype(jnp.int32), axis=1)
    owner_hot = segment[:, None] == jnp.arange(seq_lengths.shape[0], dtype=jnp.int32)[None, :]
    position = row_index - jnp.sum(jnp.where(owner_hot, seq_starts[None, :], 0), axis=1)
    return (segment, position)


def rotary_tables(position, head_size):
    half_size = head_size // 2
    freq_index = jnp.arange(half_size, dtype=jnp.float32)
    inverse = jnp.exp(freq_index * (-2.0 / head_size) * math.log(ROPE_BASE))
    angles = position.astype(jnp.float32)[:, None] * inverse[None, :]
    return (jnp.cos(angles), jnp.sin(angles))


def rotate(vectors, cosine, sine_part):
    half_size = vectors.shape[-1] // 2
    lower_half = vectors[..., :half_size]
    upper_half = vectors[..., half_size:]
    cosine = cosine[:, None, :]
    sine_part = sine_part[:, None, :]
    return jnp.concatenate(
        [
            lower_half * cosine - upper_half * sine_part,
            upper_half * cosine + lower_half * sine_part,
        ],
        axis=-1,
    )


def unrotate(vectors, cosine, sine_part):
    half_size = vectors.shape[-1] // 2
    lower_half = vectors[..., :half_size]
    upper_half = vectors[..., half_size:]
    cosine = cosine[:, None, :]
    sine_part = sine_part[:, None, :]
    return jnp.concatenate(
        [
            lower_half * cosine + upper_half * sine_part,
            upper_half * cosine - lower_half * sine_part,
        ],
        axis=-1,
    )


def visible(segment, row_valid):
    row_index = jnp.arange(segment.shape[0], dtype=jnp.int32)
    same_seq = segment[:, None] == segment[None, :]
    return same_seq & (row_index[None, :] <= row_index[:, None]) & row_valid[:, None]


def product(left_side, right_side):
    return jnp.dot(left_side, right_side, preferred_element_type=jnp.float32)


def across(left_side, right_side):
    return lax.dot_general(
        left_side, right_side, (((0,), (0,)), ((), ())), preferred_element_type=jnp.float32
    )


def against(left_side, right_side):
    return lax.dot_general(
        left_side, right_side, (((1,), (1,)), ((), ())), preferred_element_type=jnp.float32
    )


def norm_back(upstream, signal, inverse, gain_vec):
    weighted = upstream * gain_vec
    gain_part = jnp.sum(upstream * signal * inverse, axis=0)
    signal_part = inverse * weighted - signal * (inverse * inverse * inverse) * jnp.mean(
        weighted * signal, axis=1, keepdims=True
    )
    return (signal_part, gain_part)


def fetch_attention(first_gain, query_weight, key_weight, value_weight, output_weight, second_gain):
    return (
        lax.all_gather(first_gain, ("dp", "tensor"), axis=0, tiled=True),
        lax.all_gather(query_weight, ("dp", "tensor"), axis=0, tiled=True),
        lax.all_gather(key_weight, ("dp", "tensor"), axis=0, tiled=True),
        lax.all_gather(value_weight, ("dp", "tensor"), axis=0, tiled=True),
        lax.all_gather(output_weight, ("dp", "tensor"), axis=0, tiled=True),
        lax.all_gather(second_gain, ("dp", "tensor"), axis=0, tiled=True),
    )


def fetch_mlp(gate_weight, up_weight, down_weight):
    return (
        lax.all_gather(gate_weight, "dp", axis=0, tiled=True),
        lax.all_gather(up_weight, "dp", axis=0, tiled=True),
        lax.all_gather(down_weight, "dp", axis=1, tiled=True),
    )


def reduce_attention(new_parts):
    return (
        lax.psum_scatter(new_parts[0], ("dp", "tensor"), scatter_dimension=0, tiled=True),
        lax.psum_scatter(new_parts[1], ("dp", "tensor"), scatter_dimension=0, tiled=True),
        lax.psum_scatter(new_parts[2], ("dp", "tensor"), scatter_dimension=0, tiled=True),
        lax.psum_scatter(new_parts[3], ("dp", "tensor"), scatter_dimension=0, tiled=True),
        lax.psum_scatter(new_parts[4], ("dp", "tensor"), scatter_dimension=0, tiled=True),
        lax.psum_scatter(new_parts[5], ("dp", "tensor"), scatter_dimension=0, tiled=True),
    )


def reduce_mlp(new_parts):
    return (
        lax.psum_scatter(new_parts[0], "dp", scatter_dimension=0, tiled=True),
        lax.psum_scatter(new_parts[1], "dp", scatter_dimension=0, tiled=True),
        lax.psum_scatter(new_parts[2], "dp", scatter_dimension=1, tiled=True),
    )


def accumulate(running, new_parts):
    if running is None:
        return tuple(new_parts)
    return tuple((earlier + latest for earlier, latest in zip(running, new_parts)))


def forward_block(inputs, seq_lengths, attn_full, mlp_full):
    first_gain, query_weight, key_weight, value_weight, output_weight, second_gain = attn_full
    gate_weight, up_weight, down_weight = mlp_full
    row_count = inputs.shape[0]
    group_size = HEADS // KV_HEADS
    factor = 1.0 / math.sqrt(HEAD)
    segment, position = pack_layout(seq_lengths, row_count)
    allowed = visible(segment, segment < SLOTS - 1)
    cosine, sine_part = rotary_tables(position, HEAD)
    first_scale = lax.rsqrt(jnp.mean(inputs * inputs, axis=1, keepdims=True) + EPSILON)
    normed_first = (inputs * first_scale * first_gain.astype(jnp.float32)).astype(jnp.bfloat16)
    queries = rotate(
        product(normed_first, query_weight).reshape(row_count, HEADS, HEAD), cosine, sine_part
    )
    queries = queries.astype(jnp.bfloat16).reshape(row_count, KV_HEADS, group_size, HEAD)
    key_vecs = rotate(
        product(normed_first, key_weight).reshape(row_count, KV_HEADS, HEAD), cosine, sine_part
    ).astype(jnp.bfloat16)
    values = (
        product(normed_first, value_weight).astype(jnp.bfloat16).reshape(row_count, KV_HEADS, HEAD)
    )
    scores = (
        jnp.einsum("qhgd,khd->hgqk", queries, key_vecs, preferred_element_type=jnp.float32) * factor
    )
    row_peak = jnp.max(jnp.where(allowed, scores, NEG_LARGE), axis=-1, keepdims=True)
    raised = jnp.where(allowed, jnp.exp(jnp.where(allowed, scores - row_peak, 0.0)), 0.0)
    totals = jnp.sum(raised, axis=-1, keepdims=True)
    safe_totals = jnp.where(totals > 0, totals, 1.0)
    log_total = row_peak + jnp.log(safe_totals)
    attn_probs = (raised / safe_totals).astype(jnp.bfloat16)
    blended = jnp.einsum("hgqk,khd->qhgd", attn_probs, values, preferred_element_type=jnp.float32)
    attended = blended.reshape(row_count, HEADS * HEAD).astype(jnp.bfloat16)
    middle = inputs + product(attended, output_weight)
    second_scale = lax.rsqrt(jnp.mean(middle * middle, axis=1, keepdims=True) + EPSILON)
    normed_second = (middle * second_scale * second_gain.astype(jnp.float32)).astype(jnp.bfloat16)
    gathered = lax.all_gather(normed_second, "tensor", axis=0, tiled=True)
    gate_pre = product(gathered, gate_weight)
    up_pre = product(gathered, up_weight)
    hidden = (jax.nn.silu(gate_pre) * up_pre).astype(jnp.bfloat16)
    layer_sum = middle + lax.psum_scatter(
        product(hidden, down_weight).astype(jnp.bfloat16), "tensor", scatter_dimension=0, tiled=True
    ).astype(jnp.float32)
    saved_state = (
        inputs,
        first_scale,
        normed_first,
        allowed,
        cosine,
        sine_part,
        queries,
        key_vecs,
        values,
        log_total,
        attended,
        middle,
        second_scale,
        gathered,
        gate_pre,
        up_pre,
        hidden,
    )
    return (layer_sum, saved_state)


def backward_block(upstream_low, saved_state, attn_full, mlp_full):
    (
        inputs,
        first_scale,
        normed_first,
        allowed,
        cosine,
        sine_part,
        queries,
        key_vecs,
        values,
        log_total,
        attended,
        middle,
        second_scale,
        gathered,
        gate_pre,
        up_pre,
        hidden,
    ) = saved_state
    first_gain, query_weight, key_weight, value_weight, output_weight, second_gain = attn_full
    gate_weight, up_weight, down_weight = mlp_full
    row_count = inputs.shape[0]
    group_size = HEADS // KV_HEADS
    factor = 1.0 / math.sqrt(HEAD)
    upstream = upstream_low.astype(jnp.float32)
    grad_gathered = lax.all_gather(upstream_low, "tensor", axis=0, tiled=True)
    hidden_grad = against(grad_gathered, down_weight)
    sig_gate = jax.nn.sigmoid(gate_pre)
    gate_grad = (hidden_grad * up_pre * sig_gate * (1.0 + gate_pre * (1.0 - sig_gate))).astype(
        jnp.bfloat16
    )
    up_grad = (hidden_grad * gate_pre * sig_gate).astype(jnp.bfloat16)
    mlp_parts = (
        across(gathered, gate_grad),
        across(gathered, up_grad),
        across(hidden, grad_gathered),
    )
    second_grad = lax.psum_scatter(
        against(gate_grad, gate_weight) + against(up_grad, up_weight),
        "tensor",
        scatter_dimension=0,
        tiled=True,
    )
    middle_part, second_gain_grad = norm_back(
        second_grad, middle, second_scale, second_gain.astype(jnp.float32)
    )
    middle_grad = upstream + middle_part
    middle_low = middle_grad.astype(jnp.bfloat16)
    output_part = across(attended, middle_low)
    attended_grad = (
        against(middle_low, output_weight)
        .astype(jnp.bfloat16)
        .reshape(row_count, KV_HEADS, group_size, HEAD)
    )
    scores = (
        jnp.einsum("qhgd,khd->hgqk", queries, key_vecs, preferred_element_type=jnp.float32) * factor
    )
    attn_probs = jnp.where(allowed, jnp.exp(jnp.where(allowed, scores - log_total, 0.0)), 0.0)
    prob_grad = jnp.einsum(
        "qhgd,khd->hgqk", attended_grad, values, preferred_element_type=jnp.float32
    )
    delta_sum = jnp.sum(attn_probs * prob_grad, axis=-1, keepdims=True)
    score_grad = (attn_probs * (prob_grad - delta_sum)).astype(jnp.bfloat16)
    value_grad = jnp.einsum(
        "hgqk,qhgd->khd",
        attn_probs.astype(jnp.bfloat16),
        attended_grad,
        preferred_element_type=jnp.float32,
    )
    value_grad = value_grad.astype(jnp.bfloat16).reshape(row_count, KV_HEADS * HEAD)
    query_rot_grad = (
        jnp.einsum("hgqk,khd->qhgd", score_grad, key_vecs, preferred_element_type=jnp.float32)
        * factor
    )
    key_rot_grad = (
        jnp.einsum("hgqk,qhgd->khd", score_grad, queries, preferred_element_type=jnp.float32)
        * factor
    )
    query_grad = (
        unrotate(query_rot_grad.reshape(row_count, HEADS, HEAD), cosine, sine_part)
        .astype(jnp.bfloat16)
        .reshape(row_count, HEADS * HEAD)
    )
    key_grad = (
        unrotate(key_rot_grad, cosine, sine_part)
        .astype(jnp.bfloat16)
        .reshape(row_count, KV_HEADS * HEAD)
    )
    first_grad = (
        against(query_grad, query_weight)
        + against(key_grad, key_weight)
        + against(value_grad, value_weight)
    )
    input_part, first_gain_grad = norm_back(
        first_grad, inputs, first_scale, first_gain.astype(jnp.float32)
    )
    input_grad = middle_grad + input_part
    attn_parts = (
        first_gain_grad,
        across(normed_first, query_grad),
        across(normed_first, key_grad),
        across(normed_first, value_grad),
        output_part,
        second_gain_grad,
    )
    return (input_grad, attn_parts, mlp_parts)


def per_device(
    tokens,
    lengths,
    first_gain,
    query_weight,
    key_weight,
    value_weight,
    output_weight,
    second_gain,
    gate_weight,
    up_weight,
    down_weight,
    cotangent,
):
    micro_count = tokens.shape[0]
    outputs = []
    input_grads = []
    attn_total = None
    mlp_total = None
    for step_index in range(micro_count):
        attn_full = fetch_attention(
            first_gain, query_weight, key_weight, value_weight, output_weight, second_gain
        )
        mlp_full = fetch_mlp(gate_weight, up_weight, down_weight)
        layer_sum, saved_state = forward_block(
            tokens[step_index].astype(jnp.float32), lengths[step_index, 0], attn_full, mlp_full
        )
        outputs.append(layer_sum.astype(jnp.bfloat16))
        input_grad, attn_parts, mlp_parts = backward_block(
            cotangent[step_index], saved_state, attn_full, mlp_full
        )
        input_grads.append(input_grad)
        attn_parts = reduce_attention(attn_parts)
        mlp_parts = reduce_mlp(mlp_parts)
        attn_total = accumulate(attn_total, attn_parts)
        mlp_total = accumulate(mlp_total, mlp_parts)
    return (
        jnp.stack(outputs),
        jnp.stack(input_grads),
        attn_total[0],
        attn_total[1],
        attn_total[2],
        attn_total[3],
        attn_total[4],
        attn_total[5],
        mlp_total[0],
        mlp_total[1],
        mlp_total[2],
    )


def solution(mesh):
    placed = (
        P(None, ("dp", "tensor"), None),
        P(None, ("dp", "tensor"), None),
        P(("dp", "tensor")),
        P(("dp", "tensor"), None),
        P(("dp", "tensor"), None),
        P(("dp", "tensor"), None),
        P(("dp", "tensor"), None),
        P(("dp", "tensor")),
        P("dp", "tensor"),
        P("dp", "tensor"),
        P("tensor", "dp"),
        P(None, ("dp", "tensor"), None),
    )
    return jax.shard_map(
        per_device,
        mesh=mesh,
        in_specs=placed,
        out_specs=(
            P(None, ("dp", "tensor"), None),
            P(None, ("dp", "tensor"), None),
            P(("dp", "tensor")),
            P(("dp", "tensor"), None),
            P(("dp", "tensor"), None),
            P(("dp", "tensor"), None),
            P(("dp", "tensor"), None),
            P(("dp", "tensor")),
            P("dp", "tensor"),
            P("dp", "tensor"),
            P("tensor", "dp"),
        ),
        check_vma=False,
    )
```

profile of v0, /device:TPU:0, one launch (start us, length us, event | category | flops | bytes accessed | tf_op | source)
XLA Modules:
  0.0 1699.0 jit_solution(15163263010389915065)
XLA Ops:
  14.5 42.2 %all-reduce.5 = (bf16[1536]{0:T(1024)(128)(2,1)S(1)}, bf16[1536]{0:T(1024)(128)(2,1)S(1)}) all-reduce(bf16[1536]{0:T(1024)(128)(2,1)S(1)} %dynamic-update-slice, bf16[1536]{0:T(1024)(128)(2,1)S(1)} %dynamic-update-slice.1), channel_id=1, replica_groups=mesh['dp'=8,'tensor'=4] {'dp','tensor'}, use_global_device_ids=true, to_apply=%add | all-reduce | flops 3072 | bytes 12288
  61.2 9.6 all-gather.17.cloned.1.call-done
  74.0 55.8 %all-gather.19.cloned.1.call-done = bf16[1536,768]{1,0:T(8,128)(2,1)} async-done(((bf16[48,768]{1,0:T(8,128)(2,1)}), bf16[1536,768]{1,0:T(8,128)(2,1)}) %all-gather.19.cloned.1.call-update) | async-done | bytes 2359312 | tf_op jit(solution)/shard_map/all_gather | solution.py:99
  135.1 60.2 %all-gather.21.cloned.1.call-done = bf16[1536,1536]{1,0:T(8,128)(2,1)} async-done(((bf16[48,1536]{1,0:T(8,128)(2,1)}), bf16[1536,1536]{1,0:T(8,128)(2,1)}) %all-gather.21.cloned.1.call-update) | async-done | bytes 4718608 | tf_op jit(solution)/shard_map/all_gather | solution.py:98
  207.8 52.7 %all-gather.23.cloned.1.call-done = bf16[1536,1536]{1,0:T(8,128)(2,1)} async-done(((bf16[48,1536]{1,0:T(8,128)(2,1)}), bf16[1536,1536]{1,0:T(8,128)(2,1)}) %all-gather.23.cloned.1.call-update) | async-done | bytes 4718608 | tf_op jit(solution)/shard_map/all_gather | solution.py:101
  268.4 53.5 %all-gather.29.cloned.1.call-done = bf16[1536,1024]{1,0:T(8,128)(2,1)} async-done(((bf16[192,1024]{1,0:T(8,128)(2,1)}), bf16[1536,1024]{1,0:T(8,128)(2,1)}) %all-gather.29.cloned.1.call-update) | async-done | bytes 3145744 | tf_op jit(solution)/shard_map/all_gather | solution.py:109
  321.9 20.3 %all-gather.25.cloned.1.call-done = bf16[512,1536]{1,0:T(8,128)(2,1)} async-done(((bf16[128,1536]{1,0:T(8,128)(2,1)}), bf16[512,1536]{1,0:T(8,128)(2,1)}) %all-gather.25.cloned.1.call-update) | async-done | bytes 1572880 | tf_op jit(solution)/shard_map/all_gather | solution.py:174
  347.7 57.1 %all-gather.27.cloned.1.call-done = bf16[1536,1024]{1,0:T(8,128)(2,1)} async-done(((bf16[192,1024]{1,0:T(8,128)(2,1)}), bf16[1536,1024]{1,0:T(8,128)(2,1)}) %all-gather.27.cloned.1.call-update) | async-done | bytes 3145744 | tf_op jit(solution)/shard_map/all_gather | solution.py:108
  409.9 15.4 all-gather.37.cloned.1.call-done
  425.3 62.7 %all-gather.31.cloned.1.call-done = bf16[1024,1536]{0,1:T(8,128)(2,1)} async-done(((bf16[1024,192]{0,1:T(8,128)(2,1)}), bf16[1024,1536]{0,1:T(8,128)(2,1)}) %all-gather.31.cloned.1.call-update) | async-done | bytes 3145744 | tf_op jit(solution)/shard_map/all_gather | solution.py:110
  531.1 35.7 %reduce-scatter.20.cloned.1.call-done = f32[128,1536]{1,0:T(8,128)} async-done(((f32[512,1536]{1,0:T(8,128)}), f32[128,1536]{1,0:T(8,128)}) %reduce-scatter.20.cloned.1.call-update) | async-done | bytes 786448 | tf_op jit(solution)/shard_map/reduce_scatter | solution.py:241
  572.2 17.7 %all-gather.35.cloned.1.call-done = bf16[512,1536]{1,0:T(8,128)(2,1)} async-done(((bf16[128,1536]{1,0:T(8,128)(2,1)}), bf16[512,1536]{1,0:T(8,128)(2,1)}) %all-gather.35.cloned.1.call-update) | async-done | bytes 1572880 | tf_op jit(solution)/shard_map/all_gather | solution.py:174
  598.6 13.0 all-gather.41.cloned.1.call-done
  641.6 12.3 all-gather.39.cloned.1.call-done
  684.4 31.3 %reduce-scatter.16.cloned.1.call-done = bf16[128,1536]{1,0:T(8,128)(2,1)} async-done(((bf16[512,1536]{1,0:T(8,128)(2,1)}), bf16[128,1536]{1,0:T(8,128)(2,1)}) %reduce-scatter.16.cloned.1.call-update) | async-done | bytes 393232 | tf_op jit(solution)/shard_map/reduce_scatter | solution.py:178
  715.7 40.4 %reduce-scatter.22.cloned.1.call-done = f32[128,1536]{1,0:T(8,128)} async-done(((f32[512,1536]{1,0:T(8,128)}), f32[128,1536]{1,0:T(8,128)}) %reduce-scatter.22.cloned.1.call-update) | async-done | bytes 786448 | tf_op jit(solution)/shard_map/reduce_scatter | solution.py:241
  756.1 40.7 %reduce-scatter.24.cloned.1.call-done = f32[128,1536]{1,0:T(8,128)} async-done(((f32[512,1536]{1,0:T(8,128)}), f32[128,1536]{1,0:T(8,128)}) %reduce-scatter.24.cloned.1.call-update) | async-done | bytes 786448 | tf_op jit(solution)/shard_map/reduce_scatter | solution.py:241
  909.6 39.9 %all-reduce.4 = (f32[1536]{0:T(1024)}, f32[1536]{0:T(1024)}) all-reduce(f32[1536]{0:T(1024)} %add_add_fusion.6, f32[1536]{0:T(1024)S(1)} %copy-done.131), channel_id=29, replica_groups=mesh['dp'=8,'tensor'=4] {'dp','tensor'}, use_global_device_ids=true, to_apply=%region_37.38.clone | all-reduce | flops 3072 | bytes 24576
  960.3 85.1 %reduce-scatter.28.cloned.1.call-done = f32[48,768]{1,0:T(8,128)} async-done(((f32[1536,768]{1,0:T(8,128)}), f32[48,768]{1,0:T(8,128)}) %reduce-scatter.28.cloned.1.call-update) | async-done | bytes 147472 | tf_op jit(solution)/shard_map/reduce_scatter | solution.py:118
  1045.4 121.3 %reduce-scatter.38.cloned.1.call-done = f32[1024,192]{0,1:T(8,128)} async-done(((f32[1024,1536]{0,1:T(8,128)}), f32[1024,192]{0,1:T(8,128)}) %reduce-scatter.38.cloned.1.call-update) | async-done | bytes 786448 | tf_op jit(solution)/shard_map/reduce_scatter | solution.py:129
  1166.7 121.3 %reduce-scatter.36.cloned.1.call-done = f32[192,1024]{1,0:T(8,128)} async-done(((f32[1536,1024]{1,0:T(8,128)}), f32[192,1024]{1,0:T(8,128)}) %reduce-scatter.36.cloned.1.call-update) | async-done | bytes 786448 | tf_op jit(solution)/shard_map/reduce_scatter | solution.py:128
  1288.0 121.1 %reduce-scatter.34.cloned.1.call-done = f32[192,1024]{1,0:T(8,128)} async-done(((f32[1536,1024]{1,0:T(8,128)}), f32[192,1024]{1,0:T(8,128)}) %reduce-scatter.34.cloned.1.call-update) | async-done | bytes 786448 | tf_op jit(solution)/shard_map/reduce_scatter | solution.py:127
  1409.2 141.2 %reduce-scatter.32.cloned.1.call-done = f32[48,1536]{1,0:T(8,128)} async-done(((f32[1536,1536]{1,0:T(8,128)}), f32[48,1536]{1,0:T(8,128)}) %reduce-scatter.32.cloned.1.call-update) | async-done | bytes 294928 | tf_op jit(solution)/shard_map/reduce_scatter | solution.py:120
  1550.3 142.0 %reduce-scatter.26.cloned.1.call-done = f32[48,1536]{1,0:T(8,128)} async-done(((f32[1536,1536]{1,0:T(8,128)}), f32[48,1536]{1,0:T(8,128)}) %reduce-scatter.26.cloned.1.call-update) | async-done | bytes 294928 | tf_op jit(solution)/shard_map/reduce_scatter | solution.py:117
  (615 shorter events, 289.8 us)
Async XLA Ops:
  7.2 63.7 %all-gather.17.cloned.1.call-start = ((), (), s32[]{:S(2)}) async-start(), calls=%async_computation.13 | async-start | bytes 2433024 | tf_op jit(solution)/shard_map/all_gather | solution.py:100
  7.9 121.9 %all-gather.19.cloned.1.call-start = ((), (), s32[]{:S(2)}) async-start(), calls=%async_computation.14 | async-start | bytes 2433024 | tf_op jit(solution)/shard_map/all_gather | solution.py:99
  8.7 186.6 %all-gather.21.cloned.1.call-start = ((), (), s32[]{:S(2)}) async-start(), calls=%async_computation.15 | async-start | bytes 4866048 | tf_op jit(solution)/shard_map/all_gather | solution.py:98
  9.4 251.1 %all-gather.23.cloned.1.call-start = ((), (), s32[]{:S(2)}) async-start(), calls=%async_computation.16 | async-start | bytes 4866048 | tf_op jit(solution)/shard_map/all_gather | solution.py:101
  10.0 311.9 %all-gather.29.cloned.1.call-start = ((), (), s32[]{:S(2)}) async-start(), calls=%async_computation.19 | async-start | bytes 3538944 | tf_op jit(solution)/shard_map/all_gather | solution.py:109
  10.6 331.6 %all-gather.25.cloned.1.call-start = ((), (), s32[]{:S(2)}) async-start(), calls=%async_computation.17 | async-start | bytes 1966080 | tf_op jit(solution)/shard_map/all_gather | solution.py:174
  265.2 139.6 %all-gather.27.cloned.1.call-start = ((), (), s32[]{:S(2)}) async-start(), calls=%async_computation.18 | async-start | bytes 3538944 | tf_op jit(solution)/shard_map/all_gather | solution.py:108
  266.0 159.3 %all-gather.37.cloned.1.call-start = ((), (), s32[]{:S(2)}) async-start(), calls=%async_computation.29 | async-start | bytes 1966080 | tf_op jit(solution)/shard_map/all_gather | solution.py:229
  267.1 220.8 %all-gather.31.cloned.1.call-start = ((), (), s32[]{:S(2)}) async-start(), calls=%async_computation.20 | async-start | bytes 3538944 | tf_op jit(solution)/shard_map/all_gather | solution.py:110
  267.9 263.2 %reduce-scatter.14.cloned.1.call-start = ((), (), s32[]{:S(2)}) async-start(), calls=%async_computation.21 | async-start | bytes 1966080 | tf_op jit(solution)/shard_map/reduce_scatter | solution.py:178
  499.2 67.6 %reduce-scatter.20.cloned.1.call-start = ((), (), s32[]{:S(2)}) async-start(), calls=%async_computation.26 | async-start | bytes 3932160 | tf_op jit(solution)/shard_map/reduce_scatter | solution.py:241
  507.9 81.9 %all-gather.35.cloned.1.call-start = ((), (), s32[]{:S(2)}) async-start(), calls=%async_computation.24 | async-start | bytes 1966080 | tf_op jit(solution)/shard_map/all_gather | solution.py:174
  571.3 82.5 %all-gather.39.cloned.1.call-start = ((), (), s32[]{:S(2)}) async-start(), calls=%async_computation.30 | async-start | bytes 1966080 | tf_op jit(solution)/shard_map/all_gather | solution.py:229
  571.9 112.5 %reduce-scatter.18.cloned.1.call-start = ((), (), s32[]{:S(2)}) async-start(), calls=%async_computation.25 | async-start | bytes 1966080 | tf_op jit(solution)/shard_map/reduce_scatter | solution.py:178
  623.4 92.3 %reduce-scatter.16.cloned.1.call-start = ((), (), s32[]{:S(2)}) async-start(), calls=%async_computation.23 | async-start | bytes 1966080 | tf_op jit(solution)/shard_map/reduce_scatter | solution.py:178
  665.4 90.7 %reduce-scatter.22.cloned.1.call-start = ((), (), s32[]{:S(2)}) async-start(), calls=%async_computation.27 | async-start | bytes 3932160 | tf_op jit(solution)/shard_map/reduce_scatter | solution.py:241
  673.7 123.1 %reduce-scatter.24.cloned.1.call-start = ((), (), s32[]{:S(2)}) async-start(), calls=%async_computation.28 | async-start | bytes 3932160 | tf_op jit(solution)/shard_map/reduce_scatter | solution.py:241
  681.6 278.7 %reduce-scatter.30.cloned.1.call-start = ((), (), s32[]{:S(2)}) async-start(), calls=%async_computation.34 | async-start | bytes 4866048 | tf_op jit(solution)/shard_map/reduce_scatter | solution.py:119
  825.1 220.4 %reduce-scatter.28.cloned.1.call-start = ((), (), s32[]{:S(2)}) async-start(), calls=%async_computation.33 | async-start | bytes 4866048 | tf_op jit(solution)/shard_map/reduce_scatter | solution.py:118
  837.9 328.8 %reduce-scatter.38.cloned.1.call-start = ((), (), s32[]{:S(2)}) async-start(), calls=%async_computation.38 | async-start | bytes 7077888 | tf_op jit(solution)/shard_map/reduce_scatter | solution.py:129
  848.5 439.5 %reduce-scatter.36.cloned.1.call-start = ((), (), s32[]{:S(2)}) async-start(), calls=%async_computation.37 | async-start | bytes 7077888 | tf_op jit(solution)/shard_map/reduce_scatter | solution.py:128
  859.3 549.8 %reduce-scatter.34.cloned.1.call-start = ((), (), s32[]{:S(2)}) async-start(), calls=%async_computation.36 | async-start | bytes 7077888 | tf_op jit(solution)/shard_map/reduce_scatter | solution.py:127
  869.7 680.6 %reduce-scatter.32.cloned.1.call-start = ((), (), s32[]{:S(2)}) async-start(), calls=%async_computation.35 | async-start | bytes 9732096 | tf_op jit(solution)/shard_map/reduce_scatter | solution.py:120
  879.8 812.5 %reduce-scatter.26.cloned.1.call-start = ((), (), s32[]{:S(2)}) async-start(), calls=%async_computation.32 | async-start | bytes 9732096 | tf_op jit(solution)/shard_map/reduce_scatter | solution.py:117
  (196 other events, 1816.7 us)
Sparse Core Ops, SparseCore 0:
  10.9 59.9 all-gather.16
  73.8 56.0 all-gather.18
  132.7 62.5 all-gather.20
  198.1 62.4 all-gather.22
  262.6 59.2 all-gather.28
  344.3 60.4 all-gather.26
  427.5 60.4 all-gather.30
  499.3 26.7 reduce-scatter.13
  528.8 37.9 reduce-scatter.19
  570.1 19.6 all-gather.34
  591.9 19.6 all-gather.40
  613.1 19.6 all-gather.32
  634.2 19.6 all-gather.38
  656.2 28.1 reduce-scatter.17
  687.6 28.1 reduce-scatter.15
  718.1 37.9 reduce-scatter.21
  758.8 37.9 reduce-scatter.23
  825.2 107.0 reduce-scatter.29
  939.2 106.1 reduce-scatter.27
  1049.6 117.0 reduce-scatter.37
  1170.9 117.0 reduce-scatter.35
  1292.0 117.0 reduce-scatter.33
  1415.6 134.6 reduce-scatter.31
  1557.6 134.5 reduce-scatter.25
  (2 shorter events, 36.4 us)
where the time goes:
time: 1710 us; the launch traced here: 1700 us
  waiting for transfers between devices  1330 us (78%)
  matrix products  200 us (12%)
  blocking collectives  82.1 us (5%)
  other arithmetic  37.4 us (2%)
  local copies, waits for them, and re-layouts  32.3 us (2%)
    reduce_scatter x1, waiting for transfers between devices, reduce_attention(): lax.psum_scatter(new_parts[1], ('dp', 'tensor'), scatter_dimension=0, til...  142 us
    reduce_scatter x1, waiting for transfers between devices, reduce_attention(): lax.psum_scatter(new_parts[4], ('dp', 'tensor'), scatter_dimension=0, til...  141 us
    reduce_scatter x1, waiting for transfers between devices, reduce_mlp(): lax.psum_scatter(new_parts[1], 'dp', scatter_dimension=0, tiled=True)  121 us
    reduce_scatter x1, waiting for transfers between devices, reduce_mlp(): lax.psum_scatter(new_parts[2], 'dp', scatter_dimension=1, tiled=True)  121 us
    reduce_scatter x1, waiting for transfers between devices, reduce_mlp(): lax.psum_scatter(new_parts[0], 'dp', scatter_dimension=0, tiled=True)  121 us
    reduce_scatter x3, waiting for transfers between devices, backward_block(): lax.psum_scatter(against(gate_grad, gate_weight) + against(up_grad, up_we...  117 us
    reduce_scatter x1, waiting for transfers between devices, reduce_attention(): lax.psum_scatter(new_parts[2], ('dp', 'tensor'), scatter_dimension=0, til...  85.1 us
    unnamed x2, blocking collectives  82.1 us
  transfers between devices with their start and end apart: 26, of which 24 were waited for; matrix products, arithmetic and copies ran while one was open for 13% of the time, Pallas kernels for 0%

commit v1 on v0

--- a/solution.py
+++ b/solution.py
@@ -171,7 +171,21 @@
     middle = inputs + product(attended, output_weight)
     second_scale = lax.rsqrt(jnp.mean(middle * middle, axis=1, keepdims=True) + EPSILON)
     normed_second = (middle * second_scale * second_gain.astype(jnp.float32)).astype(jnp.bfloat16)
-    gathered = lax.all_gather(normed_second, "tensor", axis=0, tiled=True)
+    n_chips = jax.lax.axis_size("tensor")
+    all_blocks = [normed_second]
+    for p in [*range(n_chips - 1)]:
+        all_blocks.append(
+            jax.lax.ppermute(
+                all_blocks[-1],
+                axis_name="tensor",
+                perm=[(m, (m + 1) % n_chips) for m in range(n_chips)],
+            )
+        )
+    gathered = jnp.roll(
+        jnp.concatenate(all_blocks[::-1], 0),
+        (jax.lax.axis_index("tensor") + 1) * normed_second.shape[0],
+        0,
+    )
     gate_pre = product(gathered, gate_weight)
     up_pre = product(gathered, up_weight)
     hidden = (jax.nn.silu(gate_pre) * up_pre).astype(jnp.bfloat16)

time: 1710 us -> 1660 us (0.971)
  waiting for transfers between devices: 1330 us -> 1250 us
  other arithmetic: 37.4 us -> 57.4 us
    all_gather x3 -> x0, waiting for transfers between devices: 47.3 us -> none  [forward_block(): gathered = lax.all_gather(normed_second, 'tensor', axis=0, tiled=True)]
    ppermute x0 -> x9, waiting for transfers between devices: none -> 45.1 us  [forward_block(): jax.lax.ppermute(all_blocks[-1], axis_name='tensor', perm=[(m, (m + 1) %...]
    all_gather x3, waiting for transfers between devices: 40.7 us -> 0.37 us  [backward_block(): grad_gathered = lax.all_gather(upstream_low, 'tensor', axis=0, tiled=True)]
  transfers between devices with their start and end apart: 26 -> 32, of which waited for: 24 -> 24; matrix products, arithmetic and copies ran while one was open for 13% -> 14% of each run, Pallas kernels for 0% -> 0%
where the time goes in v1:
time: 1660 us; the launch traced here: 1650 us
  waiting for transfers between devices  1250 us (75%)
  matrix products  190 us (11%)
  blocking collectives  82.2 us (5%)
  other arithmetic  57.4 us (3%)
  local copies, waits for them, and re-layouts  38.9 us (2%)
  between operations  17.1 us (1%)
  starting transfers between devices  16.6 us (1%)
    reduce_scatter x1, waiting for transfers between devices, reduce_attention(): lax.psum_scatter(new_parts[1], ('dp', 'tensor'), scatter_dimension=0, til...  142 us
    reduce_scatter x1, waiting for transfers between devices, reduce_attention(): lax.psum_scatter(new_parts[4], ('dp', 'tensor'), scatter_dimension=0, til...  141 us
    reduce_scatter x1, waiting for transfers between devices, reduce_mlp(): lax.psum_scatter(new_parts[2], 'dp', scatter_dimension=1, tiled=True)  121 us
    reduce_scatter x1, waiting for transfers between devices, reduce_mlp(): lax.psum_scatter(new_parts[0], 'dp', scatter_dimension=0, tiled=True)  121 us
    reduce_scatter x1, waiting for transfers between devices, reduce_mlp(): lax.psum_scatter(new_parts[1], 'dp', scatter_dimension=0, tiled=True)  121 us
    reduce_scatter x3, waiting for transfers between devices, backward_block(): lax.psum_scatter(against(gate_grad, gate_weight) + against(up_grad, up_we...  100 us
    reduce_scatter x1, waiting for transfers between devices, reduce_attention(): lax.psum_scatter(new_parts[2], ('dp', 'tensor'), scatter_dimension=0, til...  86.2 us
    unnamed x2, blocking collectives  82.2 us
  transfers between devices with their start and end apart: 32, of which 24 were waited for; matrix products, arithmetic and copies ran while one was open for 14% of the time, Pallas kernels for 0%

profile of v1, /device:TPU:0, one launch (start us, length us, event | category | flops | bytes accessed | tf_op | source)
XLA Modules:
  0.0 1648.0 jit_solution(7400816539513562640)
XLA Ops:
  17.8 42.1 %all-reduce.5 = (bf16[1536]{0:T(1024)(128)(2,1)S(1)}, bf16[1536]{0:T(1024)(128)(2,1)S(1)}) all-reduce(bf16[1536]{0:T(1024)(128)(2,1)S(1)} %dynamic-update-slice, bf16[1536]{0:T(1024)(128)(2,1)S(1)} %dynamic-update-slice.1), channel_id=1, replica_groups=mesh['dp'=8,'tensor'=4] {'dp','tensor'}, use_global_device_ids=true, to_apply=%add | all-reduce | flops 3072 | bytes 12288
  61.6 9.5 all-gather.14.cloned.1.call-done
  74.1 55.9 %all-gather.16.cloned.1.call-done = bf16[1536,768]{1,0:T(8,128)(2,1)} async-done(((bf16[48,768]{1,0:T(8,128)(2,1)}), bf16[1536,768]{1,0:T(8,128)(2,1)}) %all-gather.16.cloned.1.call-update) | async-done | bytes 2359312 | tf_op jit(solution)/shard_map/all_gather | solution.py:99
  135.2 60.3 %all-gather.18.cloned.1.call-done = bf16[1536,1536]{1,0:T(8,128)(2,1)} async-done(((bf16[48,1536]{1,0:T(8,128)(2,1)}), bf16[1536,1536]{1,0:T(8,128)(2,1)}) %all-gather.18.cloned.1.call-update) | async-done | bytes 4718608 | tf_op jit(solution)/shard_map/all_gather | solution.py:98
  209.4 51.3 %all-gather.20.cloned.1.call-done = bf16[1536,1536]{1,0:T(8,128)(2,1)} async-done(((bf16[48,1536]{1,0:T(8,128)(2,1)}), bf16[1536,1536]{1,0:T(8,128)(2,1)}) %all-gather.20.cloned.1.call-update) | async-done | bytes 4718608 | tf_op jit(solution)/shard_map/all_gather | solution.py:101
  266.2 10.5 collective-permute-done
  277.9 8.0 collective-permute-done.1
  286.1 60.3 %all-gather.26.cloned.1.call-done = bf16[1024,1536]{0,1:T(8,128)(2,1)} async-done(((bf16[1024,192]{0,1:T(8,128)(2,1)}), bf16[1024,1536]{0,1:T(8,128)(2,1)}) %all-gather.26.cloned.1.call-update) | async-done | bytes 3145744 | tf_op jit(solution)/shard_map/all_gather | solution.py:110
  358.5 49.2 %all-gather.24.cloned.1.call-done = bf16[1536,1024]{1,0:T(8,128)(2,1)} async-done(((bf16[192,1024]{1,0:T(8,128)(2,1)}), bf16[1536,1024]{1,0:T(8,128)(2,1)}) %all-gather.24.cloned.1.call-update) | async-done | bytes 3145744 | tf_op jit(solution)/shard_map/all_gather | solution.py:109
  413.2 55.8 %all-gather.22.cloned.1.call-done = bf16[1536,1024]{1,0:T(8,128)(2,1)} async-done(((bf16[192,1024]{1,0:T(8,128)(2,1)}), bf16[1536,1024]{1,0:T(8,128)(2,1)}) %all-gather.22.cloned.1.call-update) | async-done | bytes 3145744 | tf_op jit(solution)/shard_map/all_gather | solution.py:108
  469.0 7.7 multiply_convert_fusion.4
  489.2 11.7 all-gather.30.cloned.1.call-start
  528.9 19.2 %reduce-scatter.20.cloned.1.call-done = f32[128,1536]{1,0:T(8,128)} async-done(((f32[512,1536]{1,0:T(8,128)}), f32[128,1536]{1,0:T(8,128)}) %reduce-scatter.20.cloned.1.call-update) | async-done | bytes 786448 | tf_op jit(solution)/shard_map/reduce_scatter | solution.py:255
  559.6 12.5 collective-permute-done.7
  637.1 19.6 %reduce-scatter.16.cloned.1.call-done = bf16[128,1536]{1,0:T(8,128)(2,1)} async-done(((bf16[512,1536]{1,0:T(8,128)(2,1)}), bf16[128,1536]{1,0:T(8,128)(2,1)}) %reduce-scatter.16.cloned.1.call-update) | async-done | bytes 393232 | tf_op jit(solution)/shard_map/reduce_scatter | solution.py:192
  656.7 40.3 %reduce-scatter.22.cloned.1.call-done = f32[128,1536]{1,0:T(8,128)} async-done(((f32[512,1536]{1,0:T(8,128)}), f32[128,1536]{1,0:T(8,128)}) %reduce-scatter.22.cloned.1.call-update) | async-done | bytes 786448 | tf_op jit(solution)/shard_map/reduce_scatter | solution.py:255
  697.1 40.5 %reduce-scatter.24.cloned.1.call-done = f32[128,1536]{1,0:T(8,128)} async-done(((f32[512,1536]{1,0:T(8,128)}), f32[128,1536]{1,0:T(8,128)}) %reduce-scatter.24.cloned.1.call-update) | async-done | bytes 786448 | tf_op jit(solution)/shard_map/reduce_scatter | solution.py:255
  857.0 40.0 %all-reduce.4 = (f32[1536]{0:T(1024)}, f32[1536]{0:T(1024)}) all-reduce(f32[1536]{0:T(1024)} %add_add_fusion.6, f32[1536]{0:T(1024)S(1)} %copy-done.136), channel_id=29, replica_groups=mesh['dp'=8,'tensor'=4] {'dp','tensor'}, use_global_device_ids=true, to_apply=%region_37.39.clone | all-reduce | flops 3072 | bytes 24576
  907.8 86.2 %reduce-scatter.28.cloned.1.call-done = f32[48,768]{1,0:T(8,128)} async-done(((f32[1536,768]{1,0:T(8,128)}), f32[48,768]{1,0:T(8,128)}) %reduce-scatter.28.cloned.1.call-update) | async-done | bytes 147472 | tf_op jit(solution)/shard_map/reduce_scatter | solution.py:118
  993.9 121.3 %reduce-scatter.38.cloned.1.call-done = f32[1024,192]{0,1:T(8,128)} async-done(((f32[1024,1536]{0,1:T(8,128)}), f32[1024,192]{0,1:T(8,128)}) %reduce-scatter.38.cloned.1.call-update) | async-done | bytes 786448 | tf_op jit(solution)/shard_map/reduce_scatter | solution.py:129
  1115.2 121.1 %reduce-scatter.36.cloned.1.call-done = f32[192,1024]{1,0:T(8,128)} async-done(((f32[1536,1024]{1,0:T(8,128)}), f32[192,1024]{1,0:T(8,128)}) %reduce-scatter.36.cloned.1.call-update) | async-done | bytes 786448 | tf_op jit(solution)/shard_map/reduce_scatter | solution.py:128
  1236.4 121.3 %reduce-scatter.34.cloned.1.call-done = f32[192,1024]{1,0:T(8,128)} async-done(((f32[1536,1024]{1,0:T(8,128)}), f32[192,1024]{1,0:T(8,128)}) %reduce-scatter.34.cloned.1.call-update) | async-done | bytes 786448 | tf_op jit(solution)/shard_map/reduce_scatter | solution.py:127
  1357.7 141.0 %reduce-scatter.32.cloned.1.call-done = f32[48,1536]{1,0:T(8,128)} async-done(((f32[1536,1536]{1,0:T(8,128)}), f32[48,1536]{1,0:T(8,128)}) %reduce-scatter.32.cloned.1.call-update) | async-done | bytes 294928 | tf_op jit(solution)/shard_map/reduce_scatter | solution.py:120
  1498.7 142.4 %reduce-scatter.26.cloned.1.call-done = f32[48,1536]{1,0:T(8,128)} async-done(((f32[1536,1536]{1,0:T(8,128)}), f32[48,1536]{1,0:T(8,128)}) %reduce-scatter.26.cloned.1.call-update) | async-done | bytes 294928 | tf_op jit(solution)/shard_map/reduce_scatter | solution.py:117
  (619 shorter events, 302.9 us)
Async XLA Ops:
  7.2 63.9 %all-gather.14.cloned.1.call-start = ((), (), s32[]{:S(2)}) async-start(), calls=%async_computation.13 | async-start | bytes 2433024 | tf_op jit(solution)/shard_map/all_gather | solution.py:100
  8.0 122.1 %all-gather.16.cloned.1.call-start = ((), (), s32[]{:S(2)}) async-start(), calls=%async_computation.14 | async-start | bytes 2433024 | tf_op jit(solution)/shard_map/all_gather | solution.py:99
  8.7 186.8 %all-gather.18.cloned.1.call-start = ((), (), s32[]{:S(2)}) async-start(), calls=%async_computation.15 | async-start | bytes 4866048 | tf_op jit(solution)/shard_map/all_gather | solution.py:98
  9.4 251.3 %all-gather.20.cloned.1.call-start = ((), (), s32[]{:S(2)}) async-start(), calls=%async_computation.16 | async-start | bytes 4866048 | tf_op jit(solution)/shard_map/all_gather | solution.py:101
  10.0 276.1 %all-gather.28.cloned.1.call-start = ((), (), s32[]{:S(2)}) async-start(), calls=%async_computation.26 | async-start | bytes 1966080 | tf_op jit(solution)/shard_map/all_gather | solution.py:243
  12.4 334.0 %all-gather.26.cloned.1.call-start = ((), (), s32[]{:S(2)}) async-start(), calls=%async_computation.19 | async-start | bytes 3538944 | tf_op jit(solution)/shard_map/all_gather | solution.py:110
  13.0 394.7 %all-gather.24.cloned.1.call-start = ((), (), s32[]{:S(2)}) async-start(), calls=%async_computation.18 | async-start | bytes 3538944 | tf_op jit(solution)/shard_map/all_gather | solution.py:109
  13.7 455.3 %all-gather.22.cloned.1.call-start = ((), (), s32[]{:S(2)}) async-start(), calls=%async_computation.17 | async-start | bytes 3538944 | tf_op jit(solution)/shard_map/all_gather | solution.py:108
  14.5 514.4 %reduce-scatter.14.cloned.1.call-start = ((), (), s32[]{:S(2)}) async-start(), calls=%async_computation.20 | async-start | bytes 1966080 | tf_op jit(solution)/shard_map/reduce_scatter | solution.py:192
  285.9 66.1 %collective-permute-start.2 = (bf16[128,1536]{1,0:T(8,128)(2,1)}, bf16[128,1536]{1,0:T(8,128)(2,1)}, u32[]{:S(2)}, u32[]{:S(2)}) collective-permute-start(bf16[128,1536]{1,0:T(8,128)(2,1)} %collective-permute-done.1), channel_id=1, source_target_pairs={{0,1},{1,2},{2,3},{3,0},{4,5},{5,6},{6,7},{7,4},{8,9},{9,10},{10,1... | collective-permute-start | bytes 1179656 | tf_op jit(solution)/shard_map/ppermute | solution.py:178
  480.6 67.5 %reduce-scatter.20.cloned.1.call-start = ((), (), s32[]{:S(2)}) async-start(), calls=%async_computation.23 | async-start | bytes 3932160 | tf_op jit(solution)/shard_map/reduce_scatter | solution.py:255
  488.4 84.0 %all-gather.32.cloned.1.call-start = ((), (), s32[]{:S(2)}) async-start(), calls=%async_computation.28 | async-start | bytes 1966080 | tf_op jit(solution)/shard_map/all_gather | solution.py:243
  489.2 106.8 %all-gather.30.cloned.1.call-start = ((), (), s32[]{:S(2)}) async-start(), calls=%async_computation.27 | async-start | bytes 1966080 | tf_op jit(solution)/shard_map/all_gather | solution.py:243
  559.1 78.0 %reduce-scatter.18.cloned.1.call-start = ((), (), s32[]{:S(2)}) async-start(), calls=%async_computation.22 | async-start | bytes 1966080 | tf_op jit(solution)/shard_map/reduce_scatter | solution.py:192
  595.4 61.3 %reduce-scatter.16.cloned.1.call-start = ((), (), s32[]{:S(2)}) async-start(), calls=%async_computation.21 | async-start | bytes 1966080 | tf_op jit(solution)/shard_map/reduce_scatter | solution.py:192
  619.9 77.2 %reduce-scatter.22.cloned.1.call-start = ((), (), s32[]{:S(2)}) async-start(), calls=%async_computation.24 | async-start | bytes 3932160 | tf_op jit(solution)/shard_map/reduce_scatter | solution.py:255
  627.8 109.8 %reduce-scatter.24.cloned.1.call-start = ((), (), s32[]{:S(2)}) async-start(), calls=%async_computation.25 | async-start | bytes 3932160 | tf_op jit(solution)/shard_map/reduce_scatter | solution.py:255
  635.8 271.9 %reduce-scatter.30.cloned.1.call-start = ((), (), s32[]{:S(2)}) async-start(), calls=%async_computation.31 | async-start | bytes 4866048 | tf_op jit(solution)/shard_map/reduce_scatter | solution.py:119
  773.9 220.0 %reduce-scatter.28.cloned.1.call-start = ((), (), s32[]{:S(2)}) async-start(), calls=%async_computation.30 | async-start | bytes 4866048 | tf_op jit(solution)/shard_map/reduce_scatter | solution.py:118
  786.6 328.6 %reduce-scatter.38.cloned.1.call-start = ((), (), s32[]{:S(2)}) async-start(), calls=%async_computation.35 | async-start | bytes 7077888 | tf_op jit(solution)/shard_map/reduce_scatter | solution.py:129
  797.2 439.2 %reduce-scatter.36.cloned.1.call-start = ((), (), s32[]{:S(2)}) async-start(), calls=%async_computation.34 | async-start | bytes 7077888 | tf_op jit(solution)/shard_map/reduce_scatter | solution.py:128
  807.8 549.9 %reduce-scatter.34.cloned.1.call-start = ((), (), s32[]{:S(2)}) async-start(), calls=%async_computation.33 | async-start | bytes 7077888 | tf_op jit(solution)/shard_map/reduce_scatter | solution.py:127
  818.3 680.4 %reduce-scatter.32.cloned.1.call-start = ((), (), s32[]{:S(2)}) async-start(), calls=%async_computation.32 | async-start | bytes 9732096 | tf_op jit(solution)/shard_map/reduce_scatter | solution.py:120
  827.4 813.7 %reduce-scatter.26.cloned.1.call-start = ((), (), s32[]{:S(2)}) async-start(), calls=%async_computation.29 | async-start | bytes 9732096 | tf_op jit(solution)/shard_map/reduce_scatter | solution.py:117
  (198 other events, 1265.9 us)
Sparse Core Ops, SparseCore 0:
  11.0 60.1 all-gather.13
  74.0 55.9 all-gather.15
  133.0 62.5 all-gather.17
  198.3 62.4 all-gather.19
  262.7 21.0 all-gather.27
  285.9 60.4 all-gather.25
  348.6 59.0 all-gather.23
  409.9 59.0 all-gather.21
  480.8 26.7 reduce-scatter.13
  510.2 37.9 reduce-scatter.19
  549.7 22.7 all-gather.31
  573.9 20.7 all-gather.29
  597.2 28.1 reduce-scatter.17
  628.5 28.1 reduce-scatter.15
  659.1 37.9 reduce-scatter.21
  699.6 37.9 reduce-scatter.23
  774.0 107.2 reduce-scatter.29
  888.1 105.7 reduce-scatter.27
  998.1 117.1 reduce-scatter.37
  1119.2 117.0 reduce-scatter.35
  1240.5 117.0 reduce-scatter.33
  1364.1 134.4 reduce-scatter.31
  1506.1 134.8 reduce-scatter.25
